TPU v7x, 128 devices: a whole 4x4x4 slice. The times are simulated.
128 devices in a mesh: dp: 16 (over z, x_lo, core), space: 8 (over x_hi, y).
Axes of the slice: x: 4 (x_hi: 2, x_lo: 2; x = x_hi * 2 + x_lo), y: 4, z: 4, core: 2. Of those that a mesh axis runs over, the one named last changes fastest.
Arguments:
- features: bfloat16 [16, 128, 64, 1024], P('dp', 'space'), may hold values from -6 to 6
- target: bfloat16 [16, 128, 64, 1024], P('dp', 'space'), may hold values from -6 to 6
- anchors: int32 [16, 2], P('dp'), may hold values from 0 to 64512
- w_first: bfloat16 [3, 3, 64, 64], replicated, may hold values from -0.25 to 0.25
- b_first: float32 [64], replicated, may hold values from -3 to 3
- w_second: bfloat16 [3, 3, 64, 64], replicated, may hold values from -0.25 to 0.25
- b_second: float32 [64], replicated, may hold values from -3 to 3
Outputs:
- back_input: bfloat16 [16, 128, 64, 1024], P('dp', 'space')
- grad_w1: float32 [3, 3, 64, 64], replicated
- grad_b1: float32 [64], replicated
- grad_w2: float32 [3, 3, 64, 64], replicated
- grad_b2: float32 [64], replicated
All inputs are finite; a program needn't handle non-finite values.
Results may differ from a plain program's by a relative error of at most 0.0075.
Values may be sent and summed in bfloat16 or wider, within the bound.
No kernel may reach another device: no remote copies, remote signals or barrier semaphores. Data moves between devices by JAX's collectives and lax.ppermute only.
A program may use at most 128 MiB of HBM per device.

v0:
```python
import math
import jax
import jax.numpy as jnp
from jax import lax
from jax.sharding import PartitionSpec as P


def extended(value, sides, width):
    for axis, dim in sides:
        size, length = (lax.axis_size(axis), value.shape[dim])
        up = [(i, (i + 1) % size) for i in range(size - 1)]
        down = [(j, i) for i, j in up]
        last = lax.slice_in_dim(value, length - width, length, axis=dim)
        first = lax.slice_in_dim(value, 0, width, axis=dim)
        before = lax.ppermute(last, axis, up)
        after = lax.ppermute(first, axis, down)
        value = jnp.concatenate([before, value, after], axis=dim)
    return value


def shift_cols(tensor, offset):
    if offset == 0:
        return tensor
    filler = jnp.zeros(tensor.shape[:-1] + (1,), tensor.dtype)
    if offset > 0:
        return jnp.concatenate([tensor[..., 1:], filler], axis=-1)
    return jnp.concatenate([filler, tensor[..., :-1]], axis=-1)


def unfold(padded):
    inner = padded.shape[1] - 2
    pieces = [
        shift_cols(padded[:, row_off : row_off + inner], col_off - 1)
        for row_off in range(3)
        for col_off in range(3)
    ]
    return jnp.concatenate(pieces, axis=2)


def unfold_back(padded):
    inner = padded.shape[1] - 2
    pieces = [
        shift_cols(padded[:, 2 - row_off : 2 - row_off + inner], 1 - col_off)
        for row_off in range(3)
        for col_off in range(3)
    ]
    return jnp.concatenate(pieces, axis=2)


def forward_matrix(kernel):
    return jnp.transpose(kernel, (2, 0, 1, 3)).reshape(kernel.shape[2], -1)


def backward_matrix(kernel):
    return jnp.transpose(kernel, (3, 0, 1, 2)).reshape(kernel.shape[3], -1)


def fold_kernel(matrix):
    channels = matrix.shape[0]
    return jnp.transpose(matrix.reshape(channels, 3, 3, -1), (1, 2, 0, 3))


def coords(anchor_rows, row_ids, columns, channels):
    chan_ids = jnp.arange(channels, dtype=jnp.int32)
    periods = 4 * jnp.left_shift(jnp.ones_like(chan_ids), chan_ids % 8)
    scaled = 2.0 * math.pi / periods.astype(jnp.float32)
    row_pos = anchor_rows[:, 0][:, None, None] + row_ids[None, :, None]
    row_wave = jnp.sin(
        (row_pos % periods[None, None, :]).astype(jnp.float32) * scaled[None, None, :]
    )
    col_ids = jnp.arange(columns, dtype=jnp.int32)
    col_pos = anchor_rows[:, 1][:, None, None] + col_ids[None, None, :]
    col_wave = jnp.sin(
        (col_pos % periods[None, :, None]).astype(jnp.float32) * scaled[None, :, None]
    )
    use_rows = (chan_ids < channels // 2)[None, None, :, None]
    return jnp.where(use_rows, row_wave[..., None], col_wave[:, None])


def gelu_grad(pre_act, upstream):
    return jax.vjp(lambda inputs: jax.nn.gelu(inputs, approximate=True), pre_act)[1](upstream)[0]


def mixing(form, left, right):
    return jnp.einsum(form, left, right, preferred_element_type=jnp.float32)


def combine(pairs):
    flat_grads = jnp.concatenate([piece.reshape(-1) for pair in pairs for piece in pair])
    total = lax.psum(flat_grads, ("dp", "space"))
    results = []
    start = 0
    for pair in pairs:
        for piece in pair:
            count = piece.size
            results.append(total[start : start + count].reshape(piece.shape))
            start = start + count
    return results


def shards(features, target, anchors, w_first, b_first, w_second, b_second):
    strip_rows = features.shape[1]
    columns = features.shape[3]
    channels = features.shape[2]
    dev_index = lax.axis_index("space")
    crop_rows = strip_rows * lax.axis_size("space")
    factor = 1.0 / math.sqrt(features.shape[0] * lax.axis_size("dp") * crop_rows * columns)
    row_ids = dev_index * strip_rows + jnp.arange(strip_rows, dtype=jnp.int32)
    geo = coords(anchors, row_ids, columns, channels)
    first = (features.astype(jnp.float32) + geo).astype(jnp.bfloat16)
    bias_one = b_first[None, None, :, None]
    first_pad = extended(first, (("space", 1),), 1)
    pre_act = mixing("dk,brkw->brdw", forward_matrix(w_first), unfold(first_pad)) + bias_one
    hidden = jax.nn.gelu(pre_act, approximate=True).astype(jnp.bfloat16)
    hidden_pad = extended(hidden, (("space", 1),), 1)
    output = (
        mixing("dk,brkw->brdw", forward_matrix(w_second), unfold(hidden_pad))
        + b_second[None, None, :, None]
    )
    misfit = (output - target.astype(jnp.float32)).astype(jnp.bfloat16)
    grad_w2 = fold_kernel(mixing("brdw,brkw->dk", misfit, unfold(hidden_pad))) * factor
    grad_b2 = jnp.sum(misfit.astype(jnp.float32), axis=(0, 1, 3)) * factor
    misfit_pad = extended(misfit, (("space", 1),), 1)
    back_hidden = mixing("ck,brkw->brcw", backward_matrix(w_second), unfold_back(misfit_pad))
    slope = gelu_grad(pre_act, back_hidden).astype(jnp.bfloat16)
    grad_w1 = fold_kernel(mixing("brdw,brkw->dk", slope, unfold(first_pad))) * factor
    grad_b1 = jnp.sum(slope.astype(jnp.float32), axis=(0, 1, 3)) * factor
    slope_pad = extended(slope, (("space", 1),), 1)
    back_input = mixing("ck,brkw->brcw", backward_matrix(w_first), unfold_back(slope_pad)).astype(
        jnp.bfloat16
    )
    grad_w2, grad_b2, grad_w1, grad_b1 = combine([(grad_w2, grad_b2), (grad_w1, grad_b1)])
    return (back_input, grad_w1, grad_b1, grad_w2, grad_b2)


def solution(mesh):
    in_specs = (
        P("dp", "space", None, None),
        P("dp", "space", None, None),
        P("dp", None),
        P(),
        P(),
        P(),
        P(),
    )
    out_specs = (P("dp", "space", None, None), P(), P(), P(), P())
    return jax.shard_map(shards, mesh=mesh, in_specs=in_specs, out_specs=out_specs, check_vma=False)
```

profile of v0, /device:TPU:1, one launch (start us, length us, event | category | flops | bytes accessed | tf_op | source)
XLA Modules:
  0.0 301.8 jit_solution(5083959459954517360)
XLA Ops:
  7.3 1.3 fusion.122
  10.2 3.5 %fusion.106 = f32[64,1024]{1,0:T(8,128)S(1)} fusion(f32[64]{0:T(128)S(1)} %convert_divide_fusion, s32[64]{0:T(128)S(1)} %compare_select_fusion, s32[1024]{0:T(1024)S(1)} %iota_add_fusion, pred[64]{0:T(512)(128)(4,1)S(1)} %broadcast_compare_fusion), kind=kLoop, calls=%fused_computation.138 | loop fusion | flops 589824 | bytes 266816 | tf_op jit(solution)/shard_map/sin | solution.py:73
  13.6 2.1 add_convert_fusion
  15.8 1.3 collective-permute-start.1
  17.1 4.8 %collective-permute-start = (bf16[1,1,64,1024]{3,2,1,0:T(8,128)(2,1)S(1)}, bf16[1,1,64,1024]{3,2,1,0:T(8,128)(2,1)S(1)}, u32[]{:S(2)}, u32[]{:S(2)}) collective-permute-start(bf16[1,1,64,1024]{3,2,1,0:T(8,128)(2,1)S(1)} %get-tuple-element.28), channel_id=1, source_target_pairs={{0,1},{1,2},{2,3},{3,4},{4,5},{5,6},{6,7},{8,9},{9,10},{10,11},{11... | collective-permute-start | bytes 393224 | tf_op jit(solution)/shard_map/ppermute | solution.py:15
  27.0 1.2 pad_dynamic-update-slice_fusion.14
  29.1 1.2 pad_dynamic-update-slice_fusion.12
  31.6 8.4 %fusion.35 = (bf16[1,16,64,1024]{3,2,1,0:T(8,128)(2,1)S(1)}, f32[16,1024,64]{1,2,0:T(8,128)}) fusion(f32[64]{0:T(128)S(1)} %copy-done.6, bf16[64,576,1]{0,1,2:T(8,128)(2,1)S(1)} %bitcast.173, bf16[1,16,576,1024]{3,2,1,0:T(8,128)(2,1)S(1)} %fusion.65), kind=kOutput, calls=%fused_computation.44 | convolution fusion | flops 1218445312 | bytes 25239808 | tf_op jit(solution)/shard_map/dk,brkw->brdw/dot_general | solution.py:85
  40.0 1.3 collective-permute-start.3
  41.3 4.6 %collective-permute-start.2 = (bf16[1,1,64,1024]{3,2,1,0:T(8,128)(2,1)S(1)}, bf16[1,1,64,1024]{3,2,1,0:T(8,128)(2,1)S(1)}, u32[]{:S(2)}, u32[]{:S(2)}) collective-permute-start(bf16[1,1,64,1024]{3,2,1,0:T(8,128)(2,1)S(1)} %get-tuple-element.22), channel_id=1, source_target_pairs={{0,1},{1,2},{2,3},{3,4},{4,5},{5,6},{6,7},{8,9},{9,10},{10,11},{11... | collective-permute-start | bytes 393224 | tf_op jit(solution)/shard_map/ppermute | solution.py:15
  46.1 1.5 collective-permute-done.2
  55.1 8.4 %convert_reduce_fusion.1 = (f32[64]{0:T(128)S(1)}, bf16[1,16,64,1024]{3,2,1,0:T(8,128)(2,1)S(1)}) fusion(bf16[1,16,64,1024]{3,2,1,0:T(8,128)(2,1)} %param.8, f32[64]{0:T(128)S(1)} %copy-done.5, bf16[64,576,1]{0,1,2:T(8,128)(2,1)S(1)} %bitcast.167, bf16[1,16,576,1024]{3,2,1,0:T(8,128)(2,1)S(1)} %fusion.69), kind=kOutput, calls=%fused_computation.47 | convolution fusion | flops 1214251008 | bytes 23142912 | tf_op jit(solution)/shard_map/dk,brkw->brdw/dot_general | solution.py:85
  63.5 12.3 %fusion.92 = f32[3,3,64,64]{3,2,1,0:T(8,128)S(1)} fusion(bf16[3,3,64,16,1024]{4,2,1,0,3:T(8,128)(2,1)} %bitcast.166, bf16[1,16,64,1024]{3,2,1,0:T(8,128)(2,1)S(1)} %get-tuple-element.38), kind=kOutput, calls=%fused_computation.128 | convolution fusion | flops 1207996416 | bytes 21118976 | tf_op jit(solution)/shard_map/brdw,brkw->dk/dot_general | solution.py:85
  76.0 4.1 %collective-permute-start.5 = (bf16[1,1,64,1024]{3,2,1,0:T(8,128)(2,1)S(1)}, bf16[1,1,64,1024]{3,2,1,0:T(8,128)(2,1)S(1)}, u32[]{:S(2)}, u32[]{:S(2)}) collective-permute-start(bf16[1,1,64,1024]{3,2,1,0:T(8,128)(2,1)S(1)} %get-tuple-element.15), channel_id=1, source_target_pairs={{0,1},{1,2},{2,3},{3,4},{4,5},{5,6},{6,7},{8,9},{9,10},{10,11},{11... | collective-permute-start | bytes 393224 | tf_op jit(solution)/shard_map/ppermute | solution.py:15
  80.0 1.7 collective-permute-start.4
  82.0 5.7 %collective-permute-done.4 = bf16[1,1,64,1024]{3,2,1,0:T(8,128)(2,1)S(1)} collective-permute-done((bf16[1,1,64,1024]{3,2,1,0:T(8,128)(2,1)S(1)}, bf16[1,1,64,1024]{3,2,1,0:T(8,128)(2,1)S(1)}, u32[]{:S(2)}, u32[]{:S(2)}) %collective-permute-start.4) | collective-permute-done | bytes 131104 | tf_op jit(solution)/shard_map/ppermute | solution.py:16
  87.6 2.4 fusion.46
  90.6 1.3 fusion.71
  92.5 1.2 pad_dynamic-update-slice_fusion.5
  94.2 1.3 fusion.73
  95.5 10.1 %convert_reduce_fusion = (f32[64]{0:T(128)S(1)}, bf16[1,16,64,1024]{3,2,1,0:T(8,128)(2,1)S(1)}) fusion(f32[64]{0:T(128)S(1)} %copy-done.6, f32[16,1024,64]{1,2,0:T(8,128)} %get-tuple-element.36, bf16[64,576,1]{0,1,2:T(8,128)(2,1)S(1)} %bitcast.172, bf16[1,16,576,1024]{3,2,1,0:T(8,128)(2,1)S(1)} %fusion.73), kind=kOutput, calls=%fused_computation.46 | convolution fusion | flops 1232076800 | bytes 25240064 | tf_op jit(solution)/shard_map/ck,brkw->brcw/dot_general | solution.py:85
  105.6 12.5 %fusion.101 = f32[3,3,64,64]{3,2,1,0:T(8,128)S(1)} fusion(bf16[3,3,64,16,1024]{4,2,1,0,3:T(8,128)(2,1)} %bitcast.170, bf16[1,16,64,1024]{3,2,1,0:T(8,128)(2,1)S(1)} %get-tuple-element.40), kind=kOutput, calls=%fused_computation.131 | convolution fusion | flops 1207996416 | bytes 21118976 | tf_op jit(solution)/shard_map/brdw,brkw->dk/dot_general | solution.py:85
  118.3 7.4 %collective-permute-start.7 = (bf16[1,1,64,1024]{3,2,1,0:T(8,128)(2,1)S(1)}, bf16[1,1,64,1024]{3,2,1,0:T(8,128)(2,1)S(1)}, u32[]{:S(2)}, u32[]{:S(2)}) collective-permute-start(bf16[1,1,64,1024]{3,2,1,0:T(8,128)(2,1)S(1)} %get-tuple-element.9), channel_id=1, source_target_pairs={{0,1},{1,2},{2,3},{3,4},{4,5},{5,6},{6,7},{8,9},{9,10},{10,11},{11... | collective-permute-start | bytes 393224 | tf_op jit(solution)/shard_map/ppermute | solution.py:15
  125.7 1.3 collective-permute-start.6
  127.0 4.3 %concatenate.165 = f32[73856]{0:T(1024)} concatenate(f32[36864]{0:T(1024)S(1)} %reshape.374, f32[64]{0:T(128)S(1)} %broadcast_multiply_fusion.1, f32[36864]{0:T(1024)S(1)} %reshape.376, f32[64]{0:T(128)S(1)} %broadcast_multiply_fusion), dimensions={0} | concatenate | bytes 590848 | tf_op jit(solution)/shard_map/concatenate | solution.py:89
  131.3 4.1 %collective-permute-done.6 = bf16[1,1,64,1024]{3,2,1,0:T(8,128)(2,1)S(1)} collective-permute-done((bf16[1,1,64,1024]{3,2,1,0:T(8,128)(2,1)S(1)}, bf16[1,1,64,1024]{3,2,1,0:T(8,128)(2,1)S(1)}, u32[]{:S(2)}, u32[]{:S(2)}) %collective-permute-start.6) | collective-permute-done | bytes 131104 | tf_op jit(solution)/shard_map/ppermute | solution.py:16
  135.4 2.4 fusion.40
  138.4 1.3 fusion.75
  141.9 1.3 fusion.77
  143.2 6.7 %convert_bitcast_fusion = bf16[1,16,64,1024]{3,2,1,0:T(8,128)(2,1)} fusion(bf16[64,576,1]{0,1,2:T(8,128)(2,1)S(1)} %bitcast.169, bf16[1,16,576,1024]{3,2,1,0:T(8,128)(2,1)S(1)} %fusion.77), kind=kOutput, calls=%fused_computation.109 | convolution fusion | flops 1209008128 | bytes 21045248 | tf_op jit(solution)/shard_map/ck,brkw->brcw/dot_general | solution.py:85
  150.0 140.8 %all-reduce.26.cloned.1.call-done = f32[73856]{0:T(1024)} async-done(((f32[73856]{0:T(1024)}), f32[73856]{0:T(1024)}) %all-reduce.26.cloned.1.call-update) | async-done | bytes 295440 | tf_op jit(solution)/shard_map/psum | solution.py:90
  293.5 1.3 fusion.120
  (72 shorter events, 24.2 us)
Async XLA Ops:
  7.2 14.8 %copy-start.2 = (bf16[3,3,64,64]{3,2,1,0:T(8,128)(2,1)S(1)}, bf16[3,3,64,64]{3,2,1,0:T(8,128)(2,1)}, u32[]{:S(2)}) copy-start(bf16[3,3,64,64]{3,2,1,0:T(8,128)(2,1)} %param.10) | copy-start | bytes 221188
  7.2 283.6 %all-reduce.26.cloned.1.call-start = ((), (), s32[]{:S(2)}) async-start(), calls=%async_computation | async-start | bytes 598016 | tf_op jit(solution)/shard_map/psum | solution.py:90
  15.8 6.9 %collective-permute-start.1 = (bf16[1,1,64,1024]{3,2,1,0:T(8,128)(2,1)S(1)}, bf16[1,1,64,1024]{3,2,1,0:T(8,128)(2,1)S(1)}, u32[]{:S(2)}, u32[]{:S(2)}) collective-permute-start(bf16[1,1,64,1024]{3,2,1,0:T(8,128)(2,1)S(1)} %get-tuple-element.27), channel_id=1, source_target_pairs={{1,0},{2,1},{3,2},{4,3},{5,4},{6,5},{7,6},{9,8},{10,9},{11,10},{12... | collective-permute-start | bytes 393224 | tf_op jit(solution)/shard_map/ppermute | solution.py:16
  17.1 6.6 %collective-permute-start = (bf16[1,1,64,1024]{3,2,1,0:T(8,128)(2,1)S(1)}, bf16[1,1,64,1024]{3,2,1,0:T(8,128)(2,1)S(1)}, u32[]{:S(2)}, u32[]{:S(2)}) collective-permute-start(bf16[1,1,64,1024]{3,2,1,0:T(8,128)(2,1)S(1)} %get-tuple-element.28), channel_id=1, source_target_pairs={{0,1},{1,2},{2,3},{3,4},{4,5},{5,6},{6,7},{8,9},{9,10},{10,11},{11... | collective-permute-start | bytes 393224 | tf_op jit(solution)/shard_map/ppermute | solution.py:15
  25.9 2.3 copy-start.1
  30.2 1.4 copy-start.6
  31.6 8.4 %copy-start.3 = (bf16[1,16,576,1024]{3,2,1,0:T(8,128)(2,1)}, bf16[1,16,576,1024]{3,2,1,0:T(8,128)(2,1)S(1)}, u32[]{:S(2)}) copy-start(bf16[1,16,576,1024]{3,2,1,0:T(8,128)(2,1)S(1)} %fusion.65) | copy-start | bytes 56623108
  31.6 14.3 %copy-start.4 = (bf16[3,3,64,64]{3,2,1,0:T(8,128)(2,1)S(1)}, bf16[3,3,64,64]{3,2,1,0:T(8,128)(2,1)}, u32[]{:S(2)}) copy-start(bf16[3,3,64,64]{3,2,1,0:T(8,128)(2,1)} %param.12) | copy-start | bytes 221188
  40.0 6.1 %collective-permute-start.3 = (bf16[1,1,64,1024]{3,2,1,0:T(8,128)(2,1)S(1)}, bf16[1,1,64,1024]{3,2,1,0:T(8,128)(2,1)S(1)}, u32[]{:S(2)}, u32[]{:S(2)}) collective-permute-start(bf16[1,1,64,1024]{3,2,1,0:T(8,128)(2,1)S(1)} %get-tuple-element.21), channel_id=1, source_target_pairs={{1,0},{2,1},{3,2},{4,3},{5,4},{6,5},{7,6},{9,8},{10,9},{11,10},{12... | collective-permute-start | bytes 393224 | tf_op jit(solution)/shard_map/ppermute | solution.py:16
  41.3 6.3 %collective-permute-start.2 = (bf16[1,1,64,1024]{3,2,1,0:T(8,128)(2,1)S(1)}, bf16[1,1,64,1024]{3,2,1,0:T(8,128)(2,1)S(1)}, u32[]{:S(2)}, u32[]{:S(2)}) collective-permute-start(bf16[1,1,64,1024]{3,2,1,0:T(8,128)(2,1)S(1)} %get-tuple-element.22), channel_id=1, source_target_pairs={{0,1},{1,2},{2,3},{3,4},{4,5},{5,6},{6,7},{8,9},{9,10},{10,11},{11... | collective-permute-start | bytes 393224 | tf_op jit(solution)/shard_map/ppermute | solution.py:15
  53.8 1.3 copy-start.5
  55.1 8.4 %copy-start = (bf16[1,16,576,1024]{3,2,1,0:T(8,128)(2,1)}, bf16[1,16,576,1024]{3,2,1,0:T(8,128)(2,1)S(1)}, u32[]{:S(2)}) copy-start(bf16[1,16,576,1024]{3,2,1,0:T(8,128)(2,1)S(1)} %fusion.69) | copy-start | bytes 56623108
  76.0 6.0 %collective-permute-start.5 = (bf16[1,1,64,1024]{3,2,1,0:T(8,128)(2,1)S(1)}, bf16[1,1,64,1024]{3,2,1,0:T(8,128)(2,1)S(1)}, u32[]{:S(2)}, u32[]{:S(2)}) collective-permute-start(bf16[1,1,64,1024]{3,2,1,0:T(8,128)(2,1)S(1)} %get-tuple-element.15), channel_id=1, source_target_pairs={{0,1},{1,2},{2,3},{3,4},{4,5},{5,6},{6,7},{8,9},{9,10},{10,11},{11... | collective-permute-start | bytes 393224 | tf_op jit(solution)/shard_map/ppermute | solution.py:15
  80.0 7.6 %collective-permute-start.4 = (bf16[1,1,64,1024]{3,2,1,0:T(8,128)(2,1)S(1)}, bf16[1,1,64,1024]{3,2,1,0:T(8,128)(2,1)S(1)}, u32[]{:S(2)}, u32[]{:S(2)}) collective-permute-start(bf16[1,1,64,1024]{3,2,1,0:T(8,128)(2,1)S(1)} %get-tuple-element.16), channel_id=1, source_target_pairs={{1,0},{2,1},{3,2},{4,3},{5,4},{6,5},{7,6},{9,8},{10,9},{11,10},{12... | collective-permute-start | bytes 393224 | tf_op jit(solution)/shard_map/ppermute | solution.py:16
  118.3 13.1 %collective-permute-start.7 = (bf16[1,1,64,1024]{3,2,1,0:T(8,128)(2,1)S(1)}, bf16[1,1,64,1024]{3,2,1,0:T(8,128)(2,1)S(1)}, u32[]{:S(2)}, u32[]{:S(2)}) collective-permute-start(bf16[1,1,64,1024]{3,2,1,0:T(8,128)(2,1)S(1)} %get-tuple-element.9), channel_id=1, source_target_pairs={{0,1},{1,2},{2,3},{3,4},{4,5},{5,6},{6,7},{8,9},{9,10},{10,11},{11... | collective-permute-start | bytes 393224 | tf_op jit(solution)/shard_map/ppermute | solution.py:15
  125.7 9.7 %collective-permute-start.6 = (bf16[1,1,64,1024]{3,2,1,0:T(8,128)(2,1)S(1)}, bf16[1,1,64,1024]{3,2,1,0:T(8,128)(2,1)S(1)}, u32[]{:S(2)}, u32[]{:S(2)}) collective-permute-start(bf16[1,1,64,1024]{3,2,1,0:T(8,128)(2,1)S(1)} %get-tuple-element.10), channel_id=1, source_target_pairs={{1,0},{2,1},{3,2},{4,3},{5,4},{6,5},{7,6},{9,8},{10,9},{11,10},{12... | collective-permute-start | bytes 393224 | tf_op jit(solution)/shard_map/ppermute | solution.py:16
Sparse Core Ops, SparseCore 0:
  131.4 159.3 all-reduce.25
where the time goes:
time: 306 us; the launch traced here: 302 us
  waiting for transfers between devices  154 us (50%)
  matrix products  58.4 us (19%)
  starting transfers between devices  26.5 us (9%)
  other arithmetic  25.8 us (8%)
  local copies, waits for them, and re-layouts  22.4 us (7%)
  between operations  14.9 us (5%)
    psum x1, waiting for transfers between devices, combine(): total = lax.psum(flat_grads, ('dp', 'space'))  141 us
    dot_general x6, matrix products, mixing(): return jnp.einsum(form, left, right, preferred_element_type=jnp.float32)  58.4 us
    ppermute x4, starting transfers between devices, extended(): before = lax.ppermute(last, axis, up)  20.9 us
    unnamed x33, local copies, waits for them, and re-layouts  12.2 us
    ppermute x4, waiting for transfers between devices, extended(): after = lax.ppermute(first, axis, down)  10.4 us
    unnamed x13, other arithmetic  7.09 us
    concatenate x4, other arithmetic, extended(): value = jnp.concatenate([before, value, after], axis=dim)  6.78 us
  transfers between devices with their start and end apart: 9, of which 7 were waited for; matrix products, arithmetic and copies ran while one was open for 6% of the time, Pallas kernels for 0%

commit v1 on v0

--- a/solution.py
+++ b/solution.py
@@ -87,7 +87,7 @@
 
 def combine(pairs):
     flat_grads = jnp.concatenate([piece.reshape(-1) for pair in pairs for piece in pair])
-    total = lax.psum(flat_grads, ("dp", "space"))
+    total = lax.psum(lax.psum(flat_grads, "space"), "dp")
     results = []
     start = 0
     for pair in pairs:

time: 306 us -> 360 us (1.18)
  waiting for transfers between devices: 154 us -> 188 us
  local copies, waits for them, and re-layouts: 22.4 us -> 29 us
  matrix products: 58.4 us -> 64.9 us
  other arithmetic: 25.8 us -> 31.5 us
    psum x1 -> x2, waiting for transfers between devices: 141 us -> 175 us  [combine(): total = lax.psum(lax.psum(flat_grads, 'space'), 'dp')]
    unnamed x33, local copies, waits for them, and re-layouts: 12.2 us -> 18.7 us
    dot_general x6, matrix products: 58.4 us -> 64.9 us  [mixing(): return jnp.einsum(form, left, right, preferred_element_type=jnp.float32)]
    unnamed x13, other arithmetic: 7.09 us -> 11.3 us
  transfers between devices with their start and end apart: 9 -> 10, of which waited for: 7 -> 8; matrix products, arithmetic and copies ran while one was open for 6% -> 11% of each run, Pallas kernels for 0% -> 0%
where the time goes in v1:
time: 360 us; the launch traced here: 355 us
  waiting for transfers between devices  188 us (52%)
  matrix products  64.9 us (18%)
  other arithmetic  31.5 us (9%)
  local copies, waits for them, and re-layouts  29 us (8%)
  starting transfers between devices  26.6 us (7%)
  between operations  14.8 us (4%)
    psum x2, waiting for transfers between devices, combine(): total = lax.psum(lax.psum(flat_grads, 'space'), 'dp')  175 us
    dot_general x6, matrix products, mixing(): return jnp.einsum(form, left, right, preferred_element_type=jnp.float32)  64.9 us
    ppermute x4, starting transfers between devices, extended(): before = lax.ppermute(last, axis, up)  20.9 us
    unnamed x33, local copies, waits for them, and re-layouts  18.7 us
    unnamed x13, other arithmetic  11.3 us
    ppermute x4, waiting for transfers between devices, extended(): after = lax.ppermute(first, axis, down)  10.3 us
  transfers between devices with their start and end apart: 10, of which 8 were waited for; matrix products, arithmetic and copies ran while one was open for 11% of the time, Pallas kernels for 0%

profile of v1, /device:TPU:1, one launch (start us, length us, event | category | flops | bytes accessed | tf_op | source)
XLA Modules:
  0.0 355.2 jit_solution(2040450000284470141)
XLA Ops:
  7.3 1.3 fusion.122
  10.2 3.5 fusion.106
  13.6 2.1 add_convert_fusion
  17.1 4.8 %collective-permute-start = (bf16[1,1,64,1024]{3,2,1,0:T(8,128)(2,1)S(1)}, bf16[1,1,64,1024]{3,2,1,0:T(8,128)(2,1)S(1)}, u32[]{:S(2)}, u32[]{:S(2)}) collective-permute-start(bf16[1,1,64,1024]{3,2,1,0:T(8,128)(2,1)S(1)} %get-tuple-element.28), channel_id=1, source_target_pairs={{0,1},{1,2},{2,3},{3,4},{4,5},{5,6},{6,7},{8,9},{9,10},{10,11},{11... | collective-permute-start | bytes 393224 | tf_op jit(solution)/shard_map/ppermute | solution.py:15
  31.6 8.4 %fusion.35 = (bf16[1,16,64,1024]{3,2,1,0:T(8,128)(2,1)S(1)}, f32[16,1024,64]{1,2,0:T(8,128)}) fusion(f32[64]{0:T(128)S(1)} %copy-done.6, bf16[64,576,1]{0,1,2:T(8,128)(2,1)S(1)} %bitcast.173, bf16[1,16,576,1024]{3,2,1,0:T(8,128)(2,1)S(1)} %fusion.65), kind=kOutput, calls=%fused_computation.44 | convolution fusion | flops 1218445312 | bytes 25239808 | tf_op jit(solution)/shard_map/dk,brkw->brdw/dot_general | solution.py:85
  40.0 1.3 collective-permute-start.3
  41.3 4.6 %collective-permute-start.2 = (bf16[1,1,64,1024]{3,2,1,0:T(8,128)(2,1)S(1)}, bf16[1,1,64,1024]{3,2,1,0:T(8,128)(2,1)S(1)}, u32[]{:S(2)}, u32[]{:S(2)}) collective-permute-start(bf16[1,1,64,1024]{3,2,1,0:T(8,128)(2,1)S(1)} %get-tuple-element.22), channel_id=1, source_target_pairs={{0,1},{1,2},{2,3},{3,4},{4,5},{5,6},{6,7},{8,9},{9,10},{10,11},{11... | collective-permute-start | bytes 393224 | tf_op jit(solution)/shard_map/ppermute | solution.py:15
  46.2 1.5 collective-permute-done.2
  55.1 8.4 %convert_reduce_fusion.1 = (f32[64]{0:T(128)S(1)}, bf16[1,16,64,1024]{3,2,1,0:T(8,128)(2,1)S(1)}) fusion(bf16[1,16,64,1024]{3,2,1,0:T(8,128)(2,1)} %param.8, f32[64]{0:T(128)S(1)} %copy-done.5, bf16[64,576,1]{0,1,2:T(8,128)(2,1)S(1)} %bitcast.167, bf16[1,16,576,1024]{3,2,1,0:T(8,128)(2,1)S(1)} %fusion.69), kind=kOutput, calls=%fused_computation.47 | convolution fusion | flops 1214251008 | bytes 23142912 | tf_op jit(solution)/shard_map/dk,brkw->brdw/dot_general | solution.py:85
  63.5 12.3 %fusion.92 = f32[3,3,64,64]{3,2,1,0:T(8,128)S(1)} fusion(bf16[3,3,64,16,1024]{4,2,1,0,3:T(8,128)(2,1)} %bitcast.166, bf16[1,16,64,1024]{3,2,1,0:T(8,128)(2,1)S(1)} %get-tuple-element.38), kind=kOutput, calls=%fused_computation.128 | convolution fusion | flops 1207996416 | bytes 21118976 | tf_op jit(solution)/shard_map/brdw,brkw->dk/dot_general | solution.py:85
  76.0 4.1 %collective-permute-start.5 = (bf16[1,1,64,1024]{3,2,1,0:T(8,128)(2,1)S(1)}, bf16[1,1,64,1024]{3,2,1,0:T(8,128)(2,1)S(1)}, u32[]{:S(2)}, u32[]{:S(2)}) collective-permute-start(bf16[1,1,64,1024]{3,2,1,0:T(8,128)(2,1)S(1)} %get-tuple-element.15), channel_id=1, source_target_pairs={{0,1},{1,2},{2,3},{3,4},{4,5},{5,6},{6,7},{8,9},{9,10},{10,11},{11... | collective-permute-start | bytes 393224 | tf_op jit(solution)/shard_map/ppermute | solution.py:15
  80.1 1.8 collective-permute-start.4
  82.0 5.7 %collective-permute-done.4 = bf16[1,1,64,1024]{3,2,1,0:T(8,128)(2,1)S(1)} collective-permute-done((bf16[1,1,64,1024]{3,2,1,0:T(8,128)(2,1)S(1)}, bf16[1,1,64,1024]{3,2,1,0:T(8,128)(2,1)S(1)}, u32[]{:S(2)}, u32[]{:S(2)}) %collective-permute-start.4) | collective-permute-done | bytes 131104 | tf_op jit(solution)/shard_map/ppermute | solution.py:16
  87.6 2.4 fusion.46
  95.5 10.1 %convert_reduce_fusion = (f32[64]{0:T(128)S(1)}, bf16[1,16,64,1024]{3,2,1,0:T(8,128)(2,1)S(1)}) fusion(f32[64]{0:T(128)S(1)} %copy-done.6, f32[16,1024,64]{1,2,0:T(8,128)} %get-tuple-element.36, bf16[64,576,1]{0,1,2:T(8,128)(2,1)S(1)} %bitcast.172, bf16[1,16,576,1024]{3,2,1,0:T(8,128)(2,1)S(1)} %fusion.73), kind=kOutput, calls=%fused_computation.46 | convolution fusion | flops 1232076800 | bytes 25240064 | tf_op jit(solution)/shard_map/ck,brkw->brcw/dot_general | solution.py:85
  105.7 12.3 %fusion.101 = f32[3,3,64,64]{3,2,1,0:T(8,128)S(1)} fusion(bf16[3,3,64,16,1024]{4,2,1,0,3:T(8,128)(2,1)} %bitcast.170, bf16[1,16,64,1024]{3,2,1,0:T(8,128)(2,1)S(1)} %get-tuple-element.40), kind=kOutput, calls=%fused_computation.131 | convolution fusion | flops 1207996416 | bytes 21118976 | tf_op jit(solution)/shard_map/brdw,brkw->dk/dot_general | solution.py:85
  118.1 7.4 %collective-permute-start.7 = (bf16[1,1,64,1024]{3,2,1,0:T(8,128)(2,1)S(1)}, bf16[1,1,64,1024]{3,2,1,0:T(8,128)(2,1)S(1)}, u32[]{:S(2)}, u32[]{:S(2)}) collective-permute-start(bf16[1,1,64,1024]{3,2,1,0:T(8,128)(2,1)S(1)} %get-tuple-element.9), channel_id=1, source_target_pairs={{0,1},{1,2},{2,3},{3,4},{4,5},{5,6},{6,7},{8,9},{9,10},{10,11},{11... | collective-permute-start | bytes 393224 | tf_op jit(solution)/shard_map/ppermute | solution.py:15
  126.8 4.4 %concatenate.165 = f32[73856]{0:T(1024)} concatenate(f32[36864]{0:T(1024)S(1)} %reshape.374, f32[64]{0:T(128)S(1)} %broadcast_multiply_fusion.1, f32[36864]{0:T(1024)S(1)} %reshape.376, f32[64]{0:T(128)S(1)} %broadcast_multiply_fusion), dimensions={0} | concatenate | bytes 590848 | tf_op jit(solution)/shard_map/concatenate | solution.py:89
  131.3 4.0 %collective-permute-done.6 = bf16[1,1,64,1024]{3,2,1,0:T(8,128)(2,1)S(1)} collective-permute-done((bf16[1,1,64,1024]{3,2,1,0:T(8,128)(2,1)S(1)}, bf16[1,1,64,1024]{3,2,1,0:T(8,128)(2,1)S(1)}, u32[]{:S(2)}, u32[]{:S(2)}) %collective-permute-start.6) | collective-permute-done | bytes 131104 | tf_op jit(solution)/shard_map/ppermute | solution.py:16
  135.2 2.5 fusion.40
  137.8 1.6 pad_dynamic-update-slice_fusion.3
  139.4 1.6 fusion.42
  141.0 2.7 fusion.75
  143.7 1.7 pad_dynamic-update-slice_fusion.2
  145.4 1.6 constant_dynamic-update-slice_fusion.3
  147.0 2.5 pad_dynamic-update-slice_fusion.1
  149.4 1.6 pad_dynamic-update-slice_fusion
  151.1 1.6 fusion.39
  152.7 2.6 fusion.77
  155.3 70.4 %all-reduce.27.cloned.1.call-done = f32[73856]{0:T(1024)} async-done(((f32[73856]{0:T(1024)}), f32[73856]{0:T(1024)}) %all-reduce.27.cloned.1.call-update) | async-done | bytes 295440 | tf_op jit(solution)/shard_map/psum | solution.py:90
  225.7 13.5 %convert_bitcast_fusion = bf16[1,16,64,1024]{3,2,1,0:T(8,128)(2,1)} fusion(bf16[64,576,1]{0,1,2:T(8,128)(2,1)S(1)} %bitcast.169, bf16[1,16,576,1024]{3,2,1,0:T(8,128)(2,1)} %fusion.77), kind=kOutput, calls=%fused_computation.109 | convolution fusion | flops 1209008128 | bytes 21045248 | tf_op jit(solution)/shard_map/ck,brkw->brcw/dot_general | solution.py:85
  239.2 105.0 %all-reduce.29.cloned.1.call-done = f32[73856]{0:T(1024)} async-done(((f32[73856]{0:T(1024)}), f32[73856]{0:T(1024)}) %all-reduce.29.cloned.1.call-update) | async-done | bytes 295440 | tf_op jit(solution)/shard_map/psum | solution.py:90
  (75 shorter events, 31.3 us)
Async XLA Ops:
  7.2 14.8 %copy-start.2 = (bf16[3,3,64,64]{3,2,1,0:T(8,128)(2,1)S(1)}, bf16[3,3,64,64]{3,2,1,0:T(8,128)(2,1)}, u32[]{:S(2)}) copy-start(bf16[3,3,64,64]{3,2,1,0:T(8,128)(2,1)} %param.10) | copy-start | bytes 221188
  7.2 218.5 %all-reduce.27.cloned.1.call-start = ((), (), s32[]{:S(2)}) async-start(), calls=%async_computation | async-start | bytes 598016 | tf_op jit(solution)/shard_map/psum | solution.py:90
  15.8 6.9 %collective-permute-start.1 = (bf16[1,1,64,1024]{3,2,1,0:T(8,128)(2,1)S(1)}, bf16[1,1,64,1024]{3,2,1,0:T(8,128)(2,1)S(1)}, u32[]{:S(2)}, u32[]{:S(2)}) collective-permute-start(bf16[1,1,64,1024]{3,2,1,0:T(8,128)(2,1)S(1)} %get-tuple-element.27), channel_id=1, source_target_pairs={{1,0},{2,1},{3,2},{4,3},{5,4},{6,5},{7,6},{9,8},{10,9},{11,10},{12... | collective-permute-start | bytes 393224 | tf_op jit(solution)/shard_map/ppermute | solution.py:16
  17.1 6.6 %collective-permute-start = (bf16[1,1,64,1024]{3,2,1,0:T(8,128)(2,1)S(1)}, bf16[1,1,64,1024]{3,2,1,0:T(8,128)(2,1)S(1)}, u32[]{:S(2)}, u32[]{:S(2)}) collective-permute-start(bf16[1,1,64,1024]{3,2,1,0:T(8,128)(2,1)S(1)} %get-tuple-element.28), channel_id=1, source_target_pairs={{0,1},{1,2},{2,3},{3,4},{4,5},{5,6},{6,7},{8,9},{9,10},{10,11},{11... | collective-permute-start | bytes 393224 | tf_op jit(solution)/shard_map/ppermute | solution.py:15
  25.9 2.3 copy-start.1
  30.2 1.4 copy-start.6
  31.6 8.4 %copy-start.3 = (bf16[1,16,576,1024]{3,2,1,0:T(8,128)(2,1)}, bf16[1,16,576,1024]{3,2,1,0:T(8,128)(2,1)S(1)}, u32[]{:S(2)}) copy-start(bf16[1,16,576,1024]{3,2,1,0:T(8,128)(2,1)S(1)} %fusion.65) | copy-start | bytes 56623108
  31.6 14.3 %copy-start.4 = (bf16[3,3,64,64]{3,2,1,0:T(8,128)(2,1)S(1)}, bf16[3,3,64,64]{3,2,1,0:T(8,128)(2,1)}, u32[]{:S(2)}) copy-start(bf16[3,3,64,64]{3,2,1,0:T(8,128)(2,1)} %param.12) | copy-start | bytes 221188
  40.0 6.1 %collective-permute-start.3 = (bf16[1,1,64,1024]{3,2,1,0:T(8,128)(2,1)S(1)}, bf16[1,1,64,1024]{3,2,1,0:T(8,128)(2,1)S(1)}, u32[]{:S(2)}, u32[]{:S(2)}) collective-permute-start(bf16[1,1,64,1024]{3,2,1,0:T(8,128)(2,1)S(1)} %get-tuple-element.21), channel_id=1, source_target_pairs={{1,0},{2,1},{3,2},{4,3},{5,4},{6,5},{7,6},{9,8},{10,9},{11,10},{12... | collective-permute-start | bytes 393224 | tf_op jit(solution)/shard_map/ppermute | solution.py:16
  41.3 6.4 %collective-permute-start.2 = (bf16[1,1,64,1024]{3,2,1,0:T(8,128)(2,1)S(1)}, bf16[1,1,64,1024]{3,2,1,0:T(8,128)(2,1)S(1)}, u32[]{:S(2)}, u32[]{:S(2)}) collective-permute-start(bf16[1,1,64,1024]{3,2,1,0:T(8,128)(2,1)S(1)} %get-tuple-element.22), channel_id=1, source_target_pairs={{0,1},{1,2},{2,3},{3,4},{4,5},{5,6},{6,7},{8,9},{9,10},{10,11},{11... | collective-permute-start | bytes 393224 | tf_op jit(solution)/shard_map/ppermute | solution.py:15
  53.8 1.3 copy-start.5
  55.1 8.4 %copy-start = (bf16[1,16,576,1024]{3,2,1,0:T(8,128)(2,1)}, bf16[1,16,576,1024]{3,2,1,0:T(8,128)(2,1)S(1)}, u32[]{:S(2)}) copy-start(bf16[1,16,576,1024]{3,2,1,0:T(8,128)(2,1)S(1)} %fusion.69) | copy-start | bytes 56623108
  76.0 6.0 %collective-permute-start.5 = (bf16[1,1,64,1024]{3,2,1,0:T(8,128)(2,1)S(1)}, bf16[1,1,64,1024]{3,2,1,0:T(8,128)(2,1)S(1)}, u32[]{:S(2)}, u32[]{:S(2)}) collective-permute-start(bf16[1,1,64,1024]{3,2,1,0:T(8,128)(2,1)S(1)} %get-tuple-element.15), channel_id=1, source_target_pairs={{0,1},{1,2},{2,3},{3,4},{4,5},{5,6},{6,7},{8,9},{9,10},{10,11},{11... | collective-permute-start | bytes 393224 | tf_op jit(solution)/shard_map/ppermute | solution.py:15
  80.1 7.6 %collective-permute-start.4 = (bf16[1,1,64,1024]{3,2,1,0:T(8,128)(2,1)S(1)}, bf16[1,1,64,1024]{3,2,1,0:T(8,128)(2,1)S(1)}, u32[]{:S(2)}, u32[]{:S(2)}) collective-permute-start(bf16[1,1,64,1024]{3,2,1,0:T(8,128)(2,1)S(1)} %get-tuple-element.16), channel_id=1, source_target_pairs={{1,0},{2,1},{3,2},{4,3},{5,4},{6,5},{7,6},{9,8},{10,9},{11,10},{12... | collective-permute-start | bytes 393224 | tf_op jit(solution)/shard_map/ppermute | solution.py:16
  118.1 13.2 %collective-permute-start.7 = (bf16[1,1,64,1024]{3,2,1,0:T(8,128)(2,1)S(1)}, bf16[1,1,64,1024]{3,2,1,0:T(8,128)(2,1)S(1)}, u32[]{:S(2)}, u32[]{:S(2)}) collective-permute-start(bf16[1,1,64,1024]{3,2,1,0:T(8,128)(2,1)S(1)} %get-tuple-element.9), channel_id=1, source_target_pairs={{0,1},{1,2},{2,3},{3,4},{4,5},{5,6},{6,7},{8,9},{9,10},{10,11},{11... | collective-permute-start | bytes 393224 | tf_op jit(solution)/shard_map/ppermute | solution.py:15
  125.5 9.7 %collective-permute-start.6 = (bf16[1,1,64,1024]{3,2,1,0:T(8,128)(2,1)S(1)}, bf16[1,1,64,1024]{3,2,1,0:T(8,128)(2,1)S(1)}, u32[]{:S(2)}, u32[]{:S(2)}) collective-permute-start(bf16[1,1,64,1024]{3,2,1,0:T(8,128)(2,1)S(1)} %get-tuple-element.10), channel_id=1, source_target_pairs={{1,0},{2,1},{3,2},{4,3},{5,4},{6,5},{7,6},{9,8},{10,9},{11,10},{12... | collective-permute-start | bytes 393224 | tf_op jit(solution)/shard_map/ppermute | solution.py:16
  131.2 213.0 %all-reduce.29.cloned.1.call-start = ((), (), s32[]{:S(2)}) async-start(), calls=%async_computation.1 | async-start | bytes 598016 | tf_op jit(solution)/shard_map/psum | solution.py:90
Sparse Core Ops, SparseCore 0:
  131.3 94.3 all-reduce.26
  228.2 115.9 all-reduce.28
